TPU v7x, 32 devices: a whole 2x2x4 slice. The times are simulated.
32 devices in a mesh: rows: 8 (over z, y), group: 4 (over x, core).
Axes of the slice: x: 2, y: 2, z: 4, core: 2. Of those that a mesh axis runs over, the one named last changes fastest.
Arguments:
- inputs: bfloat16 [32, 2048, 768], P('rows', 'group'), may hold values from -6 to 6
- lengths: int32 [32, 4], P('rows'), may hold values from 1 to 1024, 2048 in all within a row
- params: float32 [6, 768], replicated
- first_moment: float32 [6, 768], replicated, may hold values from -0.0234375 to 0.0234375
- second_moment: float32 [6, 768], replicated, may hold values from 1.08506946e-07 to 8.6805557e-07
- cotangent: bfloat16 [32, 1024, 768], P('rows', 'group')
Outputs:
- output: bfloat16 [32, 1024, 768], P('rows', 'group')
- grad_inputs: bfloat16 [32, 2048, 768], P('rows', 'group')
- grad_norm: float32 [], replicated
- new_params: float32 [6, 768], replicated
- new_first: float32 [6, 768], replicated
- new_second: float32 [6, 768], replicated
Inputs may be any that keep to these rules, and one draw needn't show every extreme that they name: Each row's 4 lengths sum to 2048.
All inputs are finite; a program needn't handle non-finite values.
Results may differ from a plain program's by a relative error of at most 0.0005.
Values may be sent and summed in bfloat16 or wider, within the bound.
No kernel may reach another device: no remote copies, remote signals or barrier semaphores. Data moves between devices by JAX's collectives and lax.ppermute only.
A program may use at most 256 MiB of HBM per device.

v0:
```python
import jax
import jax.numpy as jnp
from jax import lax
from jax.sharding import PartitionSpec as P

STEP = 10
beta_one = 0.9
beta_two = 0.999
learn_rate = 0.2
decay_rate = 0.01
adam_eps = 1e-08
clip_limit = 1.0


def passed_along(value, axis, steps):
    count = lax.axis_size(axis)
    initial, last = (max(0, -steps), min(count, count - steps))
    return lax.ppermute(value, axis, [(source, source + steps) for source in range(initial, last)])


def offsets(row_lengths, positions):
    seg_ends = jnp.cumsum(row_lengths)
    seg_starts = seg_ends - row_lengths
    inside = (positions[:, None] >= seg_starts[None, :]) & (positions[:, None] < seg_ends[None, :])
    chosen_start = jnp.sum(jnp.where(inside, seg_starts[None, :], 0), axis=1)
    chosen_end = jnp.sum(jnp.where(inside, seg_ends[None, :], 0), axis=1)
    return (positions - chosen_start, chosen_end - positions)


def mix_window(padded, off_ext, rem_ext, weights):
    span = padded.shape[0] - 9
    conv_rows = span + 6
    off_conv = off_ext[3 : 3 + conv_rows]
    conv_out = jnp.zeros((conv_rows, padded.shape[1]), padded.dtype) + weights[4]
    for k in range(4):
        keep_mask = (off_conv >= k).astype(padded.dtype)[:, None]
        conv_out = conv_out + keep_mask * weights[k] * padded[3 - k : 3 - k + conv_rows]
    off_own = off_ext[6 : 6 + span]
    rem_own = rem_ext[6 : 6 + span]
    pooled = []
    for block_size in range(1, 5):
        within = off_own % block_size
        upper = jnp.minimum(block_size - within, rem_own)
        count = jnp.maximum(within + upper, 1)
        running = jnp.zeros((span, padded.shape[1]), padded.dtype)
        for j in range(1 - block_size, block_size):
            keep_mask = ((j >= -within) & (j < upper)).astype(padded.dtype)[:, None]
            running = running + keep_mask * conv_out[3 + j : 3 + j + span]
        pooled.append(running / count.astype(padded.dtype)[:, None])
    stacked = jnp.stack(pooled)
    logits = jnp.sum(stacked * weights[5], axis=2)
    largest = jnp.max(logits, axis=0, keepdims=True)
    shares = jnp.exp(logits - largest)
    shares = shares / jnp.sum(shares, axis=0, keepdims=True)
    mixed = jnp.sum(shares[:, :, None] * stacked, axis=0)
    return jnp.mean(mixed.reshape(span // 2, 2, padded.shape[1]), axis=1)


def window_info(lengths, first_position, window_rows):
    positions = lax.iota(jnp.int32, window_rows) + first_position
    return jax.vmap(lambda row_lengths: offsets(row_lengths, positions))(lengths)


def apply_rows(values, info, weights):
    return jax.vmap(
        lambda row_values, row_off, row_rem: mix_window(row_values, row_off, row_rem, weights)
    )(values, info[0], info[1])


def adam_update(grads, weights, first_old, second_old):
    first_new = beta_one * first_old + (1.0 - beta_one) * grads
    second_new = beta_two * second_old + (1.0 - beta_two) * grads * grads
    first_hat = first_new / (1.0 - beta_one**STEP)
    second_hat = second_new / (1.0 - beta_two**STEP)
    updated = weights - learn_rate * (
        first_hat / (jnp.sqrt(second_hat) + adam_eps) + decay_rate * weights
    )
    return (updated, first_new, second_new)


def per_device(inputs, lengths, params, first_moment, second_moment, cotangent):
    rows_here, length_here, features = inputs.shape
    cot_rows = cotangent.shape[1]
    before_rows, after_rows, cot_before, cot_after = (6, 3, 0, 0)
    send_up = jnp.concatenate(
        [inputs[:, length_here - before_rows :], cotangent[:, cot_rows - cot_before :]], axis=1
    )
    from_below = passed_along(send_up, "group", 1)
    send_down = jnp.concatenate([inputs[:, :after_rows], cotangent[:, :cot_after]], axis=1)
    from_above = passed_along(send_down, "group", -1)
    group_start = lax.axis_index("group") * length_here
    padded = jnp.concatenate([from_below, inputs, from_above], axis=1).astype(jnp.float32)
    main_info = window_info(lengths, group_start - 6, length_here + 9)

    def forward(values, weights):
        return apply_rows(values, main_info, weights)

    output, pullback = jax.vjp(forward, padded, params)
    grad_padded, grad_local = pullback(cotangent.astype(jnp.float32))
    grad_values = grad_padded[:, 6 : 6 + length_here]
    returned_low = passed_along(grad_padded[:, :6].astype(jnp.bfloat16), "group", -1).astype(
        jnp.float32
    )
    returned_high = passed_along(
        grad_padded[:, 6 + length_here :].astype(jnp.bfloat16), "group", 1
    ).astype(jnp.float32)
    grad_values = grad_values + jnp.concatenate(
        [jnp.zeros((rows_here, length_here - 6, features), jnp.float32), returned_low], axis=1
    )
    grad_values = grad_values + jnp.concatenate(
        [returned_high, jnp.zeros((rows_here, length_here - 3, features), jnp.float32)], axis=1
    )
    grad_params = lax.psum(grad_local, ("rows", "group"))
    grad_norm = jnp.sqrt(jnp.sum(grad_params * grad_params))
    clip_scale = jnp.minimum(1.0, clip_limit / (grad_norm + 1e-06))
    new_params, new_first, new_second = adam_update(
        grad_params * clip_scale, params, first_moment, second_moment
    )
    return (
        output.astype(jnp.bfloat16),
        grad_values.astype(jnp.bfloat16),
        grad_norm,
        new_params,
        new_first,
        new_second,
    )


def solution(mesh):
    in_specs = (P("rows", "group", None), P("rows", None), P(), P(), P(), P("rows", "group", None))
    out_specs = (P("rows", "group", None), P("rows", "group", None), P(), P(), P(), P())
    return jax.shard_map(
        per_device, mesh=mesh, in_specs=in_specs, out_specs=out_specs, check_vma=False
    )
```

profile of v0, /device:TPU:1, one launch (start us, length us, event | category | flops | bytes accessed | tf_op | source)
XLA Modules:
  0.0 251.8 jit_solution(8609651600042316704)
XLA Ops:
  0.6 0.8 slice.91
  1.4 2.0 collective-permute-start.1
  3.4 0.8 slice.90
  4.2 4.5 %collective-permute-start = (bf16[4,6,768]{2,1,0:T(8,128)(2,1)S(1)}, bf16[4,6,768]{2,1,0:T(8,128)(2,1)S(1)}, u32[]{:S(2)}, u32[]{:S(2)}) collective-permute-start(bf16[4,6,768]{2,1,0:T(8,128)(2,1)S(1)} %slice.90), channel_id=1, source_target_pairs={{0,1},{1,2},{2,3},{4,5},{5,6},{6,7},{8,9},{9,10},{10,11},{12,13},{... | collective-permute-start | bytes 110600 | tf_op jit(solution)/shard_map/ppermute | solution.py:18
  8.7 0.9 reduce_window_sum.11
  9.6 0.7 sub.50
  11.0 1.7 convert_multiply_fusion
  12.7 1.0 slice_reduce_fusion.5
  13.7 4.7 %broadcast_in_dim.41 = f32[4,256,2,768]{3,2,1,0:T(2,128)} broadcast(f32[4,256,768]{2,1,0:T(8,128)S(1)} %convert_multiply_fusion), dimensions={0,1,3} | broadcast | bytes 9437184 | tf_op jit(solution)/shard_map/transpose(jvp(vmap()))/broadcast_in_dim | solution.py:56
  18.3 8.7 %reshape.120 = f32[4,512,768]{2,1,0:T(8,128)} reshape(f32[4,256,2,768]{3,2,1,0:T(2,128)} %broadcast_in_dim.41) | data formatting | bytes 12582912 | tf_op jit(solution)/shard_map/transpose(jvp(vmap()))/reshape | solution.py:56
  27.0 0.7 maximum_convert_fusion
  27.7 4.8 %fusion.3 = f32[4,518,768]{2,1,0:T(8,128)S(1)} fusion(f32[4,521,768]{2,1,0:T(8,128)S(1)} %maximum_convert_fusion, f32[768]{0:T(1024)S(1)} %get-tuple-element.16, f32[4,518]{1,0:T(4,128)S(1)} %get-tuple-element.86, f32[768]{0:T(1024)S(1)} %get-tuple-element.17, f32[4,518]{1,0:T(4,128)S(1)} %get-tuple-element.85, f32[768]{0:T(1024)S(1)} %get-tuple-element.18, ...), kind=kLoop, calls=%fused_computation.18 | loop fusion | flops 19095552 | bytes 31874432 | tf_op jit(solution)/shard_map/jvp(vmap())/add | solution.py:37
  32.6 6.4 %divide_bitcast_fusion.1 = (f32[1,4,512,768]{3,2,1,0:T(8,128)S(1)}, f32[1,4,512,768]{3,2,1,0:T(8,128)S(1)}) fusion(f32[4,518,768]{2,1,0:T(8,128)S(1)} %fusion.3, f32[4,512]{1,0:T(4,128)S(1)} %get-tuple-element.75, f32[4,512]{1,0:T(4,128)S(1)} %get-tuple-element.72, f32[4,512]{1,0:T(4,128)S(1)} %get-tuple-element.66, f32[4,512]{1,0:T(4,128)S(1)} %get-tuple-element.35, ...), kind=kLoop, calls=%fused_computation.48 | loop fusion | flops 25165824 | bytes 44122112 | tf_op jit(solution)/shard_map/jvp(vmap())/stack | solution.py:50
  39.0 8.8 %divide_bitcast_fusion.2 = (f32[1,4,512,768]{3,2,1,0:T(8,128)S(1)}, f32[1,4,512,768]{3,2,1,0:T(8,128)}) fusion(f32[4,518,768]{2,1,0:T(8,128)S(1)} %fusion.3, f32[4,512]{1,0:T(4,128)S(1)} %get-tuple-element.87, f32[4,512]{1,0:T(4,128)S(1)} %get-tuple-element.33, f32[4,512]{1,0:T(4,128)S(1)} %get-tuple-element.76, f32[4,512]{1,0:T(4,128)S(1)} %get-tuple-element.71, ...), kind=kLoop, calls=%fused_computation.49 | loop fusion | flops 25165824 | bytes 56705024 | tf_op jit(solution)/shard_map/jvp(vmap())/stack | solution.py:50
  47.8 17.0 %multiply_reduce_fusion.1 = (f32[4,4,512]{2,0,1:T(4,128)S(1)}, f32[4,4,512]{2,0,1:T(4,128)S(1)}) fusion(f32[4,512,768]{2,1,0:T(8,128)} %reshape.120, f32[1,4,512,768]{3,2,1,0:T(8,128)} %get-tuple-element.61, f32[1,4,512,768]{3,2,1,0:T(8,128)S(1)} %get-tuple-element.63, f32[1,4,512,768]{3,2,1,0:T(8,128)S(1)} %get-tuple-element.62, ...), kind=kLoop, calls=%fused_computation.3 | loop fusion | flops 44023808 | bytes 31525888 | tf_op jit(solution)/shard_map/transpose(jvp(vmap()))/reduce_sum | solution.py:55
  65.0 14.1 %multiply_reduce_fusion = (f32[768]{0:T(1024)S(1)}, f32[4,512,768]{2,1,0:T(8,128)}) fusion(f32[4,4,512]{2,0,1:T(4,128)S(1)} %select_add_fusion, f32[1,4,512,768]{3,2,1,0:T(8,128)} %get-tuple-element.61, f32[1,4,512,768]{3,2,1,0:T(8,128)} %copy-done.2, f32[1,4,512,768]{3,2,1,0:T(8,128)} %copy-done.1, f32[1,4,512,768]{3,2,1,0:T(8,128)} %copy-done.3, ...), kind=kLoop, calls=%fused_computation.1 | loop fusion | flops 42466560 | bytes 31525888 | tf_op jit(solution)/shard_map/transpose(jvp(vmap()))/reduce_sum | solution.py:51
  79.2 11.4 %multiply_add_fusion = f32[4,4,512,768]{3,2,0,1:T(8,128)} fusion(f32[4,4,512]{2,0,1:T(4,128)S(1)} %copy.31, f32[4,512,768]{2,1,0:T(8,128)} %reshape.120, f32[4,4,512]{2,0,1:T(4,128)S(1)} %copy.30, f32[768]{0:T(1024)S(1)} %get-tuple-element.20), kind=kLoop, calls=%fused_computation.2 | loop fusion | flops 18874368 | bytes 31525888 | tf_op jit(solution)/shard_map/transpose(jvp(vmap()))/add_any | solution.py:51
  90.6 20.8 %broadcast_multiply_fusion.7 = (f32[4,512,768]{2,1,0:T(8,128)}, f32[4,512,768]{2,1,0:T(8,128)}, f32[4,512,768]{2,1,0:T(8,128)}, f32[4,512,768]{2,1,0:T(8,128)}, ...) fusion(f32[4,512]{1,0:T(4,128)S(1)} %get-tuple-element.80, ...), kind=kLoop, calls=%fused_computation.61 | loop fusion | flops 15728640 | bytes 62996480 | tf_op jit(solution)/shard_map/transpose(jvp(vmap()))/mul | solution.py:48
  111.3 20.6 %broadcast_multiply_fusion = (f32[4,512,768]{2,1,0:T(8,128)}, f32[4,512,768]{2,1,0:T(8,128)}, f32[4,512,768]{2,1,0:T(8,128)}, f32[4,512,768]{2,1,0:T(8,128)}, f3...) fusion(f32[4,512]{1,0:T(4,128)S(1)} %get-tuple-element.71, ...), kind=kLoop, calls=%fused_computation.54 | loop fusion | flops 15728640 | bytes 62996480 | tf_op jit(solution)/shard_map/transpose(jvp(vmap()))/mul | solution.py:48
  131.9 36.3 %multiply_reduce_fusion.7 = (f32[768]{0:T(1024)S(1)}, f32[768]{0:T(1024)S(1)}, f32[768]{0:T(1024)S(1)}, f32[768]{0:T(1024)S(1)}, f32[768]{0:T(1024)S(1)}, /*index=5*/f32[4,518,768]{2,1,0:T(8,128)}) fusion(f32[4,521,768]{2,1,0:T(8,128)S(1)} %bitcast.77, f32[4,518]{1,0:T(4,128)S(1)} %get-tuple-element.86, f32[4,518]{1,0:T(4,128)S(1)} %get-tuple-element.83, ...), kind=kLoop, calls=%fused_computation.22 | loop fusion | flops 44552448 | bytes 132537728 | tf_op jit(solution)/shard_map/transpose(jvp(vmap()))/reduce_sum | solution.py:37
  168.2 7.7 %multiply_multiply_fusion = (f32[4,518,768]{2,1,0:T(8,128)S(1)}, f32[4,518,768]{2,1,0:T(8,128)S(1)}, f32[4,518,768]{2,1,0:T(8,128)S(1)}, f32[4,518,768]{2,1,0:T(8,128)}) fusion(f32[4,518,768]{2,1,0:T(8,128)} %get-tuple-element.26, f32[768]{0:T(1024)S(1)} %get-tuple-element.16, f32[4,518]{1,0:T(4,128)S(1)} %get-tuple-element.86, ...), kind=kLoop, calls=%fused_computation.6 | loop fusion | flops 12730368 | bytes 31871360 | tf_op jit(solution)/shard_map/transpose(jvp(vmap()))/mul | solution.py:37
  175.9 6.8 %fusion.23 = (bf16[4,521,768]{2,1,0:T(8,128)(2,1)}, f32[4,521,768]{2,1,0:T(8,128)}) fusion(f32[4,518,768]{2,1,0:T(8,128)S(1)} %get-tuple-element.57, f32[4,518,768]{2,1,0:T(8,128)S(1)} %get-tuple-element.58, f32[4,518,768]{2,1,0:T(8,128)} %get-tuple-element.59, f32[4,518,768]{2,1,0:T(8,128)S(1)} %get-tuple-element.56), kind=kLoop, calls=%fused_computation.131 | loop fusion | flops 6402048 | bytes 35063808 | tf_op jit(solution)/shard_map/convert.5
  182.7 0.9 slice.128
  183.6 0.8 slice.127
  184.4 8.7 %bitcast_reduce_fusion = f32[4,256,768]{2,0,1:T(4,128)S(1)} fusion(f32[4,512,768]{2,1,0:T(8,128)} %get-tuple-element.7), kind=kLoop, calls=%fused_computation.46 | loop fusion | flops 786432 | bytes 9437184 | tf_op jit(solution)/shard_map/jvp(vmap())/reduce_sum | solution.py:56
  193.1 1.7 fusion.19
  194.9 38.8 %psum.7 = f32[6,768]{1,0:T(8,128)S(1)} all-reduce(f32[6,768]{1,0:T(8,128)S(1)} %pad_add_fusion.2), channel_id=1, replica_groups=mesh['rows'=8,'group'=4] {'rows','group'}, use_global_device_ids=true, to_apply=%region_18.19 | all-reduce | flops 4608 | bytes 36864 | tf_op jit(solution)/shard_map/psum | solution.py:113
  235.0 5.2 %collective-permute-start.3 = (bf16[4,3,768]{2,1,0:T(4,128)(2,1)S(1)}, bf16[4,3,768]{2,1,0:T(4,128)(2,1)S(1)}, u32[]{:S(2)}, u32[]{:S(2)}) collective-permute-start(bf16[4,3,768]{2,1,0:T(4,128)(2,1)S(1)} %slice.128), channel_id=1, source_target_pairs={{0,1},{1,2},{2,3},{4,5},{5,6},{6,7},{8,9},{9,10},{10,11},{12,13},{... | collective-permute-start | bytes 55304 | tf_op jit(solution)/shard_map/ppermute | solution.py:18
  240.2 1.9 collective-permute-start.2
  242.1 0.6 multiply_subtract_fusion
  242.8 2.8 %collective-permute-done.2 = bf16[4,6,768]{2,1,0:T(8,128)(2,1)S(1)} collective-permute-done((bf16[4,6,768]{2,1,0:T(8,128)(2,1)S(1)}, bf16[4,6,768]{2,1,0:T(8,128)(2,1)S(1)}, u32[]{:S(2)}, u32[]{:S(2)}) %collective-permute-start.2) | collective-permute-done | bytes 36896 | tf_op jit(solution)/shard_map/ppermute | solution.py:18
  245.6 5.1 %fusion.5 = bf16[4,512,768]{2,1,0:T(8,128)(2,1)} fusion(f32[4,521,768]{2,1,0:T(8,128)} %get-tuple-element.28, bf16[4,3,768]{2,1,0:T(4,128)(2,1)S(1)} %collective-permute-done.3, bf16[4,6,768]{2,1,0:T(8,128)(2,1)S(1)} %collective-permute-done.2), kind=kLoop, calls=%fused_computation.26 | loop fusion | flops 7864320 | bytes 9492480 | tf_op jit(solution)/shard_map/convert_element_type | solution.py:121
  (51 shorter events, 1.6 us)
Async XLA Ops:
  1.4 25.6 %collective-permute-start.1 = (bf16[4,3,768]{2,1,0:T(4,128)(2,1)S(1)}, bf16[4,3,768]{2,1,0:T(4,128)(2,1)S(1)}, u32[]{:S(2)}, u32[]{:S(2)}) collective-permute-start(bf16[4,3,768]{2,1,0:T(4,128)(2,1)S(1)} %slice.91), channel_id=1, source_target_pairs={{1,0},{2,1},{3,2},{5,4},{6,5},{7,6},{9,8},{10,9},{11,10},{13,12},{... | collective-permute-start | bytes 55304 | tf_op jit(solution)/shard_map/ppermute | solution.py:18
  4.2 22.8 %collective-permute-start = (bf16[4,6,768]{2,1,0:T(8,128)(2,1)S(1)}, bf16[4,6,768]{2,1,0:T(8,128)(2,1)S(1)}, u32[]{:S(2)}, u32[]{:S(2)}) collective-permute-start(bf16[4,6,768]{2,1,0:T(8,128)(2,1)S(1)} %slice.90), channel_id=1, source_target_pairs={{0,1},{1,2},{2,3},{4,5},{5,6},{6,7},{8,9},{9,10},{10,11},{12,13},{... | collective-permute-start | bytes 110600 | tf_op jit(solution)/shard_map/ppermute | solution.py:18
  18.3 8.7 %copy-start.4 = (bf16[4,512,768]{2,1,0:T(8,128)(2,1)S(1)}, bf16[4,512,768]{2,1,0:T(8,128)(2,1)}, u32[]{:S(2)}) copy-start(bf16[4,512,768]{2,1,0:T(8,128)(2,1)} %param.6) | copy-start | bytes 9437188
  27.7 4.9 %copy-start = (f32[4,521,768]{2,1,0:T(8,128)}, f32[4,521,768]{2,1,0:T(8,128)S(1)}, u32[]{:S(2)}) copy-start(f32[4,521,768]{2,1,0:T(8,128)S(1)} %maximum_convert_fusion) | copy-start | bytes 19206148
  39.0 8.8 %copy-start.1 = (f32[1,4,512,768]{3,2,1,0:T(8,128)}, f32[1,4,512,768]{3,2,1,0:T(8,128)S(1)}, u32[]{:S(2)}) copy-start(f32[1,4,512,768]{3,2,1,0:T(8,128)S(1)} %get-tuple-element.62) | copy-start | bytes 18874372
  39.0 8.8 %copy-start.2 = (f32[1,4,512,768]{3,2,1,0:T(8,128)}, f32[1,4,512,768]{3,2,1,0:T(8,128)S(1)}, u32[]{:S(2)}) copy-start(f32[1,4,512,768]{3,2,1,0:T(8,128)S(1)} %get-tuple-element.63) | copy-start | bytes 18874372
  47.8 17.0 %copy-start.3 = (f32[1,4,512,768]{3,2,1,0:T(8,128)}, f32[1,4,512,768]{3,2,1,0:T(8,128)S(1)}, u32[]{:S(2)}) copy-start(f32[1,4,512,768]{3,2,1,0:T(8,128)S(1)} %get-tuple-element.60) | copy-start | bytes 18874372
  90.6 41.3 %slice-start = ((s8[6488064]{0:T(1024)(128)(4,1)}), s8[4194304]{0:T(1024)(128)(4,1)S(1)}, s32[]{:S(2)}) async-start(s8[6488064]{0:T(1024)(128)(4,1)} %bitcast.76), calls=%async_computation | async-start | bytes 8388608
  111.3 20.6 %slice-start.1 = ((s8[6488064]{0:T(1024)(128)(4,1)}), s8[2293760]{0:T(1024)(128)(4,1)S(1)}, s32[]{:S(2)}) async-start(s8[6488064]{0:T(1024)(128)(4,1)} %bitcast.76), calls=%async_computation.1 | async-start | bytes 4587520
  184.4 57.7 %copy-start.5 = (f32[6,768]{1,0:T(8,128)S(1)}, f32[6,768]{1,0:T(8,128)}, u32[]{:S(2)}) copy-start(f32[6,768]{1,0:T(8,128)} %param.8) | copy-start | bytes 55300
  184.4 57.7 %copy-start.6 = (f32[6,768]{1,0:T(8,128)S(1)}, f32[6,768]{1,0:T(8,128)}, u32[]{:S(2)}) copy-start(f32[6,768]{1,0:T(8,128)} %param.9) | copy-start | bytes 55300
  184.4 57.7 %copy-start.7 = (f32[6,768]{1,0:T(8,128)S(1)}, f32[6,768]{1,0:T(8,128)}, u32[]{:S(2)}) copy-start(f32[6,768]{1,0:T(8,128)} %param.10) | copy-start | bytes 55300
  235.0 7.8 %collective-permute-start.3 = (bf16[4,3,768]{2,1,0:T(4,128)(2,1)S(1)}, bf16[4,3,768]{2,1,0:T(4,128)(2,1)S(1)}, u32[]{:S(2)}, u32[]{:S(2)}) collective-permute-start(bf16[4,3,768]{2,1,0:T(4,128)(2,1)S(1)} %slice.128), channel_id=1, source_target_pairs={{0,1},{1,2},{2,3},{4,5},{5,6},{6,7},{8,9},{9,10},{10,11},{12,13},{... | collective-permute-start | bytes 55304 | tf_op jit(solution)/shard_map/ppermute | solution.py:18
  240.2 5.4 %collective-permute-start.2 = (bf16[4,6,768]{2,1,0:T(8,128)(2,1)S(1)}, bf16[4,6,768]{2,1,0:T(8,128)(2,1)S(1)}, u32[]{:S(2)}, u32[]{:S(2)}) collective-permute-start(bf16[4,6,768]{2,1,0:T(8,128)(2,1)S(1)} %slice.127), channel_id=1, source_target_pairs={{1,0},{2,1},{3,2},{5,4},{6,5},{7,6},{9,8},{10,9},{11,10},{13,12},{... | collective-permute-start | bytes 110600 | tf_op jit(solution)/shard_map/ppermute | solution.py:18
where the time goes:
time: 253 us; the launch traced here: 252 us
  other arithmetic  176 us (70%)
  blocking collectives  38.8 us (15%)
  local copies, waits for them, and re-layouts  17.9 us (7%)
  starting transfers between devices  13.6 us (5%)
  waiting for transfers between devices  2.81 us (1%)
  between operations  2.81 us (1%)
    mul x2, other arithmetic, mix_window(): running = running + keep_mask * conv_out[3 + j:3 + j + span]  41.3 us
    psum x1, blocking collectives, per_device(): grad_params = lax.psum(grad_local, ('rows', 'group'))  38.8 us
    reduce_sum x1, other arithmetic, mix_window(): keep_mask * weights[k] * padded[3 - k:3 - k + conv_rows]  36.3 us
    reduce_sum x1, other arithmetic, mix_window(): mixed = jnp.sum(shares[:, :, None] * stacked, axis=0)  17 us
    another operation x2, other arithmetic, mix_window(): stacked = jnp.stack(pooled)  15.2 us
    reduce_sum x1, other arithmetic, mix_window(): logits = jnp.sum(stacked * weights[5], axis=2)  14.1 us
    ppermute x4, starting transfers between devices, passed_along(): lax.ppermute(value, axis, [(source, source + steps) for source in range(i...  13.6 us
    add_any x1, other arithmetic, mix_window(): logits = jnp.sum(stacked * weights[5], axis=2)  11.4 us
  transfers between devices with their start and end apart: 4, of which 1 were waited for; matrix products, arithmetic and copies ran while one was open for 8% of the time, Pallas kernels for 0%

commit v1 on v0

--- a/solution.py
+++ b/solution.py
@@ -110,7 +110,7 @@
     grad_values = grad_values + jnp.concatenate(
         [returned_high, jnp.zeros((rows_here, length_here - 3, features), jnp.float32)], axis=1
     )
-    grad_params = lax.psum(grad_local, ("rows", "group"))
+    grad_params = jnp.sum(lax.all_gather(grad_local, ("rows", "group")), axis=0)
     grad_norm = jnp.sqrt(jnp.sum(grad_params * grad_params))
     clip_scale = jnp.minimum(1.0, clip_limit / (grad_norm + 1e-06))
     new_params, new_first, new_second = adam_update(

time: 253 us -> 254 us (level)
  blocking collectives: 38.8 us -> 43.2 us
  starting transfers between devices: 13.6 us -> 10.8 us
    all_gather x0 -> x1, blocking collectives: none -> 43.2 us  [per_device(): grad_params = jnp.sum(lax.all_gather(grad_local, ('rows', 'group')), axis=0)]
    psum x1 -> x0, blocking collectives: 38.8 us -> none  [per_device(): grad_params = lax.psum(grad_local, ('rows', 'group'))]
    ppermute x4, starting transfers between devices: 13.6 us -> 10.8 us  [passed_along(): lax.ppermute(value, axis, [(source, source + steps) for source in range(i...]
where the time goes in v1:
time: 254 us; the launch traced here: 253 us
  other arithmetic  176 us (69%)
  blocking collectives  43.2 us (17%)
  local copies, waits for them, and re-layouts  17.9 us (7%)
  starting transfers between devices  10.8 us (4%)
  between operations  2.8 us (1%)
    all_gather x1, blocking collectives, per_device(): grad_params = jnp.sum(lax.all_gather(grad_local, ('rows', 'group')), axis=0)  43.2 us
    mul x2, other arithmetic, mix_window(): running = running + keep_mask * conv_out[3 + j:3 + j + span]  41.3 us
    reduce_sum x1, other arithmetic, mix_window(): keep_mask * weights[k] * padded[3 - k:3 - k + conv_rows]  36.3 us
    reduce_sum x1, other arithmetic, mix_window(): mixed = jnp.sum(shares[:, :, None] * stacked, axis=0)  17 us
    another operation x2, other arithmetic, mix_window(): stacked = jnp.stack(pooled)  15.2 us
    reduce_sum x1, other arithmetic, mix_window(): logits = jnp.sum(stacked * weights[5], axis=2)  14.1 us
    add_any x1, other arithmetic, mix_window(): logits = jnp.sum(stacked * weights[5], axis=2)  11.4 us
    ppermute x4, starting transfers between devices, passed_along(): lax.ppermute(value, axis, [(source, source + steps) for source in range(i...  10.8 us
  transfers between devices with their start and end apart: 4, of which 1 were waited for; matrix products, arithmetic and copies ran while one was open for 8% of the time, Pallas kernels for 0%

profile of v1, /device:TPU:1, one launch (start us, length us, event | category | flops | bytes accessed | tf_op | source)
XLA Modules:
  0.0 253.0 jit_solution(11094021499103009145)
XLA Ops:
  0.6 0.8 slice.91
  1.4 2.0 collective-permute-start.1
  3.4 0.8 slice.90
  4.2 4.5 %collective-permute-start = (bf16[4,6,768]{2,1,0:T(8,128)(2,1)S(1)}, bf16[4,6,768]{2,1,0:T(8,128)(2,1)S(1)}, u32[]{:S(2)}, u32[]{:S(2)}) collective-permute-start(bf16[4,6,768]{2,1,0:T(8,128)(2,1)S(1)} %slice.90), channel_id=1, source_target_pairs={{0,1},{1,2},{2,3},{4,5},{5,6},{6,7},{8,9},{9,10},{10,11},{12,13},{... | collective-permute-start | bytes 110600 | tf_op jit(solution)/shard_map/ppermute | solution.py:18
  8.7 0.9 reduce_window_sum.11
  9.6 0.7 sub.50
  11.0 1.7 convert_multiply_fusion
  12.7 1.0 slice_reduce_fusion.5
  13.7 4.7 %broadcast_in_dim.41 = f32[4,256,2,768]{3,2,1,0:T(2,128)} broadcast(f32[4,256,768]{2,1,0:T(8,128)S(1)} %convert_multiply_fusion), dimensions={0,1,3} | broadcast | bytes 9437184 | tf_op jit(solution)/shard_map/transpose(jvp(vmap()))/broadcast_in_dim | solution.py:56
  18.3 8.7 %reshape.120 = f32[4,512,768]{2,1,0:T(8,128)} reshape(f32[4,256,2,768]{3,2,1,0:T(2,128)} %broadcast_in_dim.41) | data formatting | bytes 12582912 | tf_op jit(solution)/shard_map/transpose(jvp(vmap()))/reshape | solution.py:56
  27.0 0.7 maximum_convert_fusion
  27.7 4.8 %fusion.3 = f32[4,518,768]{2,1,0:T(8,128)S(1)} fusion(f32[4,521,768]{2,1,0:T(8,128)S(1)} %maximum_convert_fusion, f32[768]{0:T(1024)S(1)} %get-tuple-element.16, f32[4,518]{1,0:T(4,128)S(1)} %get-tuple-element.86, f32[768]{0:T(1024)S(1)} %get-tuple-element.17, f32[4,518]{1,0:T(4,128)S(1)} %get-tuple-element.85, f32[768]{0:T(1024)S(1)} %get-tuple-element.18, ...), kind=kLoop, calls=%fused_computation.18 | loop fusion | flops 19095552 | bytes 31874432 | tf_op jit(solution)/shard_map/jvp(vmap())/add | solution.py:37
  32.6 6.4 %divide_bitcast_fusion.1 = (f32[1,4,512,768]{3,2,1,0:T(8,128)S(1)}, f32[1,4,512,768]{3,2,1,0:T(8,128)S(1)}) fusion(f32[4,518,768]{2,1,0:T(8,128)S(1)} %fusion.3, f32[4,512]{1,0:T(4,128)S(1)} %get-tuple-element.75, f32[4,512]{1,0:T(4,128)S(1)} %get-tuple-element.72, f32[4,512]{1,0:T(4,128)S(1)} %get-tuple-element.66, f32[4,512]{1,0:T(4,128)S(1)} %get-tuple-element.35, ...), kind=kLoop, calls=%fused_computation.48 | loop fusion | flops 25165824 | bytes 44122112 | tf_op jit(solution)/shard_map/jvp(vmap())/stack | solution.py:50
  39.0 8.8 %divide_bitcast_fusion.2 = (f32[1,4,512,768]{3,2,1,0:T(8,128)S(1)}, f32[1,4,512,768]{3,2,1,0:T(8,128)}) fusion(f32[4,518,768]{2,1,0:T(8,128)S(1)} %fusion.3, f32[4,512]{1,0:T(4,128)S(1)} %get-tuple-element.87, f32[4,512]{1,0:T(4,128)S(1)} %get-tuple-element.33, f32[4,512]{1,0:T(4,128)S(1)} %get-tuple-element.76, f32[4,512]{1,0:T(4,128)S(1)} %get-tuple-element.71, ...), kind=kLoop, calls=%fused_computation.49 | loop fusion | flops 25165824 | bytes 56705024 | tf_op jit(solution)/shard_map/jvp(vmap())/stack | solution.py:50
  47.8 17.0 %multiply_reduce_fusion.1 = (f32[4,4,512]{2,0,1:T(4,128)S(1)}, f32[4,4,512]{2,0,1:T(4,128)S(1)}) fusion(f32[4,512,768]{2,1,0:T(8,128)} %reshape.120, f32[1,4,512,768]{3,2,1,0:T(8,128)} %get-tuple-element.61, f32[1,4,512,768]{3,2,1,0:T(8,128)S(1)} %get-tuple-element.63, f32[1,4,512,768]{3,2,1,0:T(8,128)S(1)} %get-tuple-element.62, ...), kind=kLoop, calls=%fused_computation.3 | loop fusion | flops 44023808 | bytes 31525888 | tf_op jit(solution)/shard_map/transpose(jvp(vmap()))/reduce_sum | solution.py:55
  65.0 14.1 %multiply_reduce_fusion = (f32[768]{0:T(1024)S(1)}, f32[4,512,768]{2,1,0:T(8,128)}) fusion(f32[4,4,512]{2,0,1:T(4,128)S(1)} %select_add_fusion, f32[1,4,512,768]{3,2,1,0:T(8,128)} %get-tuple-element.61, f32[1,4,512,768]{3,2,1,0:T(8,128)} %copy-done.2, f32[1,4,512,768]{3,2,1,0:T(8,128)} %copy-done.1, f32[1,4,512,768]{3,2,1,0:T(8,128)} %copy-done.3, ...), kind=kLoop, calls=%fused_computation.1 | loop fusion | flops 42466560 | bytes 31525888 | tf_op jit(solution)/shard_map/transpose(jvp(vmap()))/reduce_sum | solution.py:51
  79.2 11.4 %multiply_add_fusion = f32[4,4,512,768]{3,2,0,1:T(8,128)} fusion(f32[4,4,512]{2,0,1:T(4,128)S(1)} %copy.36, f32[4,512,768]{2,1,0:T(8,128)} %reshape.120, f32[4,4,512]{2,0,1:T(4,128)S(1)} %copy.35, f32[768]{0:T(1024)S(1)} %get-tuple-element.20), kind=kLoop, calls=%fused_computation.2 | loop fusion | flops 18874368 | bytes 31525888 | tf_op jit(solution)/shard_map/transpose(jvp(vmap()))/add_any | solution.py:51
  90.6 20.8 %broadcast_multiply_fusion.7 = (f32[4,512,768]{2,1,0:T(8,128)}, f32[4,512,768]{2,1,0:T(8,128)}, f32[4,512,768]{2,1,0:T(8,128)}, f32[4,512,768]{2,1,0:T(8,128)}, ...) fusion(f32[4,512]{1,0:T(4,128)S(1)} %get-tuple-element.80, ...), kind=kLoop, calls=%fused_computation.61 | loop fusion | flops 15728640 | bytes 62996480 | tf_op jit(solution)/shard_map/transpose(jvp(vmap()))/mul | solution.py:48
  111.3 20.6 %broadcast_multiply_fusion = (f32[4,512,768]{2,1,0:T(8,128)}, f32[4,512,768]{2,1,0:T(8,128)}, f32[4,512,768]{2,1,0:T(8,128)}, f32[4,512,768]{2,1,0:T(8,128)}, f3...) fusion(f32[4,512]{1,0:T(4,128)S(1)} %get-tuple-element.71, ...), kind=kLoop, calls=%fused_computation.54 | loop fusion | flops 15728640 | bytes 62996480 | tf_op jit(solution)/shard_map/transpose(jvp(vmap()))/mul | solution.py:48
  131.9 36.3 %multiply_reduce_fusion.7 = (f32[768]{0:T(1024)S(1)}, f32[768]{0:T(1024)S(1)}, f32[768]{0:T(1024)S(1)}, f32[768]{0:T(1024)S(1)}, f32[768]{0:T(1024)S(1)}, /*index=5*/f32[4,518,768]{2,1,0:T(8,128)}) fusion(f32[4,521,768]{2,1,0:T(8,128)S(1)} %bitcast.79, f32[4,518]{1,0:T(4,128)S(1)} %get-tuple-element.86, f32[4,518]{1,0:T(4,128)S(1)} %get-tuple-element.83, ...), kind=kLoop, calls=%fused_computation.22 | loop fusion | flops 44552448 | bytes 132537728 | tf_op jit(solution)/shard_map/transpose(jvp(vmap()))/reduce_sum | solution.py:37
  168.2 7.7 %multiply_multiply_fusion = (f32[4,518,768]{2,1,0:T(8,128)S(1)}, f32[4,518,768]{2,1,0:T(8,128)S(1)}, f32[4,518,768]{2,1,0:T(8,128)S(1)}, f32[4,518,768]{2,1,0:T(8,128)}) fusion(f32[4,518,768]{2,1,0:T(8,128)} %get-tuple-element.26, f32[768]{0:T(1024)S(1)} %get-tuple-element.16, f32[4,518]{1,0:T(4,128)S(1)} %get-tuple-element.86, ...), kind=kLoop, calls=%fused_computation.6 | loop fusion | flops 12730368 | bytes 31871360 | tf_op jit(solution)/shard_map/transpose(jvp(vmap()))/mul | solution.py:37
  175.9 6.8 %fusion.23 = (bf16[4,521,768]{2,1,0:T(8,128)(2,1)}, f32[4,521,768]{2,1,0:T(8,128)}) fusion(f32[4,518,768]{2,1,0:T(8,128)S(1)} %get-tuple-element.57, f32[4,518,768]{2,1,0:T(8,128)S(1)} %get-tuple-element.58, f32[4,518,768]{2,1,0:T(8,128)} %get-tuple-element.59, f32[4,518,768]{2,1,0:T(8,128)S(1)} %get-tuple-element.56), kind=kLoop, calls=%fused_computation.131 | loop fusion | flops 6402048 | bytes 35063808 | tf_op jit(solution)/shard_map/convert.5
  182.7 0.9 slice.128
  183.6 0.8 slice.127
  184.4 8.7 %bitcast_reduce_fusion = f32[4,256,768]{2,0,1:T(4,128)S(1)} fusion(f32[4,512,768]{2,1,0:T(8,128)} %get-tuple-element.7), kind=kLoop, calls=%fused_computation.46 | loop fusion | flops 786432 | bytes 9437184 | tf_op jit(solution)/shard_map/jvp(vmap())/reduce_sum | solution.py:56
  193.1 1.7 fusion.19
  194.9 43.2 %all-gather.1 = f32[32,6,768]{2,1,0:T(8,128)S(1)} all-gather(f32[1,6,768]{2,1,0:T(8,128)S(1)} %add_bitcast_fusion), channel_id=2, replica_groups=mesh['rows'=8,'group'=4] {'rows','group'}, dimensions={0}, use_global_device_ids=true | all-gather | bytes 608256 | tf_op jit(solution)/shard_map/all_gather | solution.py:113
  239.5 1.9 collective-permute-start.3
  241.4 2.4 collective-permute-start.2
  243.8 0.6 multiply_subtract_fusion
  244.5 2.3 collective-permute-done.2
  246.8 5.1 %fusion.5 = bf16[4,512,768]{2,1,0:T(8,128)(2,1)} fusion(f32[4,521,768]{2,1,0:T(8,128)} %get-tuple-element.28, bf16[4,3,768]{2,1,0:T(4,128)(2,1)S(1)} %collective-permute-done.3, bf16[4,6,768]{2,1,0:T(8,128)(2,1)S(1)} %collective-permute-done.2), kind=kLoop, calls=%fused_computation.26 | loop fusion | flops 7864320 | bytes 9492480 | tf_op jit(solution)/shard_map/convert_element_type | solution.py:121
  (52 shorter events, 1.7 us)
Async XLA Ops:
  1.4 25.6 %collective-permute-start.1 = (bf16[4,3,768]{2,1,0:T(4,128)(2,1)S(1)}, bf16[4,3,768]{2,1,0:T(4,128)(2,1)S(1)}, u32[]{:S(2)}, u32[]{:S(2)}) collective-permute-start(bf16[4,3,768]{2,1,0:T(4,128)(2,1)S(1)} %slice.91), channel_id=1, source_target_pairs={{1,0},{2,1},{3,2},{5,4},{6,5},{7,6},{9,8},{10,9},{11,10},{13,12},{... | collective-permute-start | bytes 55304 | tf_op jit(solution)/shard_map/ppermute | solution.py:18
  4.2 22.8 %collective-permute-start = (bf16[4,6,768]{2,1,0:T(8,128)(2,1)S(1)}, bf16[4,6,768]{2,1,0:T(8,128)(2,1)S(1)}, u32[]{:S(2)}, u32[]{:S(2)}) collective-permute-start(bf16[4,6,768]{2,1,0:T(8,128)(2,1)S(1)} %slice.90), channel_id=1, source_target_pairs={{0,1},{1,2},{2,3},{4,5},{5,6},{6,7},{8,9},{9,10},{10,11},{12,13},{... | collective-permute-start | bytes 110600 | tf_op jit(solution)/shard_map/ppermute | solution.py:18
  18.3 8.7 %copy-start.4 = (bf16[4,512,768]{2,1,0:T(8,128)(2,1)S(1)}, bf16[4,512,768]{2,1,0:T(8,128)(2,1)}, u32[]{:S(2)}) copy-start(bf16[4,512,768]{2,1,0:T(8,128)(2,1)} %param.6) | copy-start | bytes 9437188
  27.7 4.9 %copy-start = (f32[4,521,768]{2,1,0:T(8,128)}, f32[4,521,768]{2,1,0:T(8,128)S(1)}, u32[]{:S(2)}) copy-start(f32[4,521,768]{2,1,0:T(8,128)S(1)} %maximum_convert_fusion) | copy-start | bytes 19206148
  39.0 8.8 %copy-start.1 = (f32[1,4,512,768]{3,2,1,0:T(8,128)}, f32[1,4,512,768]{3,2,1,0:T(8,128)S(1)}, u32[]{:S(2)}) copy-start(f32[1,4,512,768]{3,2,1,0:T(8,128)S(1)} %get-tuple-element.62) | copy-start | bytes 18874372
  39.0 8.8 %copy-start.2 = (f32[1,4,512,768]{3,2,1,0:T(8,128)}, f32[1,4,512,768]{3,2,1,0:T(8,128)S(1)}, u32[]{:S(2)}) copy-start(f32[1,4,512,768]{3,2,1,0:T(8,128)S(1)} %get-tuple-element.63) | copy-start | bytes 18874372
  47.8 17.0 %copy-start.3 = (f32[1,4,512,768]{3,2,1,0:T(8,128)}, f32[1,4,512,768]{3,2,1,0:T(8,128)S(1)}, u32[]{:S(2)}) copy-start(f32[1,4,512,768]{3,2,1,0:T(8,128)S(1)} %get-tuple-element.60) | copy-start | bytes 18874372
  90.6 41.3 %slice-start = ((s8[6488064]{0:T(1024)(128)(4,1)}), s8[4194304]{0:T(1024)(128)(4,1)S(1)}, s32[]{:S(2)}) async-start(s8[6488064]{0:T(1024)(128)(4,1)} %bitcast.78), calls=%async_computation | async-start | bytes 8388608
  111.3 20.6 %slice-start.1 = ((s8[6488064]{0:T(1024)(128)(4,1)}), s8[2293760]{0:T(1024)(128)(4,1)S(1)}, s32[]{:S(2)}) async-start(s8[6488064]{0:T(1024)(128)(4,1)} %bitcast.78), calls=%async_computation.1 | async-start | bytes 4587520
  184.4 59.4 %copy-start.5 = (f32[6,768]{1,0:T(8,128)S(1)}, f32[6,768]{1,0:T(8,128)}, u32[]{:S(2)}) copy-start(f32[6,768]{1,0:T(8,128)} %param.8) | copy-start | bytes 55300
  184.4 59.4 %copy-start.6 = (f32[6,768]{1,0:T(8,128)S(1)}, f32[6,768]{1,0:T(8,128)}, u32[]{:S(2)}) copy-start(f32[6,768]{1,0:T(8,128)} %param.9) | copy-start | bytes 55300
  184.4 59.4 %copy-start.7 = (f32[6,768]{1,0:T(8,128)S(1)}, f32[6,768]{1,0:T(8,128)}, u32[]{:S(2)}) copy-start(f32[6,768]{1,0:T(8,128)} %param.10) | copy-start | bytes 55300
  239.5 5.0 %collective-permute-start.3 = (bf16[4,3,768]{2,1,0:T(4,128)(2,1)S(1)}, bf16[4,3,768]{2,1,0:T(4,128)(2,1)S(1)}, u32[]{:S(2)}, u32[]{:S(2)}) collective-permute-start(bf16[4,3,768]{2,1,0:T(4,128)(2,1)S(1)} %slice.128), channel_id=1, source_target_pairs={{0,1},{1,2},{2,3},{4,5},{5,6},{6,7},{8,9},{9,10},{10,11},{12,13},{... | collective-permute-start | bytes 55304 | tf_op jit(solution)/shard_map/ppermute | solution.py:18
  241.4 5.4 %collective-permute-start.2 = (bf16[4,6,768]{2,1,0:T(8,128)(2,1)S(1)}, bf16[4,6,768]{2,1,0:T(8,128)(2,1)S(1)}, u32[]{:S(2)}, u32[]{:S(2)}) collective-permute-start(bf16[4,6,768]{2,1,0:T(8,128)(2,1)S(1)} %slice.127), channel_id=1, source_target_pairs={{1,0},{2,1},{3,2},{5,4},{6,5},{7,6},{9,8},{10,9},{11,10},{13,12},{... | collective-permute-start | bytes 110600 | tf_op jit(solution)/shard_map/ppermute | solution.py:18
